TPU v7x, 32 devices: a whole 2x2x4 slice. The times are simulated.
32 devices in a mesh: section: 4 (over y, x), dp: 8 (over z, core).
Axes of the slice: x: 2, y: 2, z: 4, core: 2. Of those that a mesh axis runs over, the one named last changes fastest.
Arguments:
- block_input: bfloat16 [48, 202, 768], P('dp'), may hold values from -6 to 6
- cotangent: bfloat16 [48, 202, 768], P('dp'), may hold values from -6 to 6
- lengths: int32 [48], P('dp'), may hold values from 1 to 202, 4848 in all
- predicted: int32 [48, 202], P('dp'), may hold values from 0 to 1, as said below
- slab: bfloat16 [4, 768, 4608], P('section')
- in_bias: float32 [4, 3072], P('section'), may hold values from -1.2 to 1.2
- norm_gain: float32 [4, 768], P('section'), may hold values from 0.5 to 1.5
- norm_bias: float32 [4, 768], P('section'), may hold values from -1.8 to 1.8
- feature_draws: int32 [12, 64, 32], replicated, may hold values from -4 to 4
Outputs:
- section_out: bfloat16 [4, 48, 202, 768], P('section', 'dp')
- section_grad: bfloat16 [4, 48, 202, 768], P('section', 'dp')
- slab_grad: float32 [4, 768, 4608], P('section', 'dp')
- bias_grad: float32 [4, 3072], P('section', 'dp')
- gain_grad: float32 [4, 768], P('section', 'dp')
- shift_grad: float32 [4, 768], P('section', 'dp')
Inputs may be any that keep to these rules, and one draw needn't show every extreme that they name: `lengths`: a molecule's tokens fill its first positions; padding positions are never read as keys. `predicted`: 1 marks a masked-prediction position; marks at padding positions count for nothing; some molecules have none.
All inputs are finite; a program needn't handle non-finite values. No bound on the sum of `lengths` on one device may be relied on, other than what follows from the above.
Results may differ from a plain program's by a relative error of at most 0.01.
Values may be sent and summed in bfloat16 or wider, within the bound.
A program may use at most 192 MiB of HBM per device.

v0:
```python
import functools

import jax
import jax.numpy as jnp
from jax import lax
from jax.experimental import pallas as pl
from jax.experimental.pallas import tpu as pltpu
from jax.sharding import PartitionSpec as P

MESH = pl.DeviceIdType.MESH
CHUNK = 384
RELAYED = (0, 3)
SPLIT = (-1, -1)
norm_epsilon = 1e-05
bf16 = jnp.bfloat16
f32 = jnp.float32


def dot(a, b):
    return lax.dot_general(a, b, (((1,), (0,)), ((), ())), preferred_element_type=f32)


def dot_cols(a, b):
    return lax.dot_general(a, b, (((1,), (1,)), ((), ())), preferred_element_type=f32)


def dot_rows(a, b):
    return lax.dot_general(a, b, (((0,), (0,)), ((), ())), preferred_element_type=f32)


def softplus(u):
    return jnp.maximum(u, 0.0) + jnp.log1p(jnp.exp(-jnp.abs(u)))


def block_mask(feature_rows, value_cols, features, head_dim):
    r = lax.broadcasted_iota(jnp.int32, (feature_rows, value_cols), 0) // features
    c = lax.broadcasted_iota(jnp.int32, (feature_rows, value_cols), 1) // head_dim
    return r == c


def flat(ref, c):
    return ref[:, :, c].reshape(ref.shape[0] * ref.shape[1], c.size)


def column(k, D):
    return pl.ds(pl.multiple_of(k * D, D), D)


def chunk_counts(cfg, odd):
    D, FF, C = cfg[3], cfg[4], cfg[-1]
    wide = FF // C
    return D // C + (wide - D // C) * odd, wide + wide * odd


def plain_gradients(cfg, odd, xin, dbr, buf_a, buf_b, g_hbm, g_sem, stage):
    D, FF, C = cfg[3], cfg[4], cfg[-1]
    first_kind, count = chunk_counts(cfg, odd)
    wide = FF // C
    own = D // C

    def store(k):
        cp = pltpu.make_async_copy(stage, g_hbm.at[:, column(k, C)], g_sem.at[0])
        cp.start()
        cp.wait()

    def one(k, carry):
        @pl.when(k < first_kind)
        def _():
            src = column(k + (wide - own) * (1 - odd), C)
            stage[...] = dot_rows(flat(dbr, pl.ds(0, D)), flat(buf_a, src))
            store(k)

        @pl.when(k >= first_kind)
        def _():
            stage[...] = dot_rows(flat(xin, pl.ds(0, D)), flat(buf_b, column(k - first_kind, C)))
            store(k)

        return carry

    lax.fori_loop(0, count, one, 0)

    @pl.when(odd == 0)
    def _():
        stage[...] = jnp.zeros_like(stage)

        def rest(k, carry):
            store(k)
            return carry

        lax.fori_loop(wide, 2 * wide, rest, 0)


def reduce_gradients(
    cfg,
    s,
    d,
    odd,
    w,
    u,
    wt,
    ut,
    xin,
    dbr,
    buf_a,
    buf_b,
    g_hbm,
    small_ref,
    small_outs,
    ready,
    keep,
    core_out,
    cross_out,
    line_out,
    final,
    small_in,
    core_send,
    core_recv,
    line_send,
    up_recv,
    down_recv,
    final_sem,
    cross_send,
    cross_recv,
    away_send,
    away_recv,
    small_send,
    small_recv,
):
    M, L, LP, D, FF, HD, FE, NS, ND, fscale, in_kernel, C = cfg
    Z = ND // 2
    B = D // ND
    R = Z * B
    K = M * LP
    wide = FF // C
    own = D // C
    fold = D // C
    keeps = keep.shape[0]
    p = lax.rem(d, 2)
    z = d // 2
    sib = d + 1 - 2 * p
    first_kind, count = chunk_counts(cfg, odd)
    cross = wide // 2
    pre = jnp.where(s == 1, cross, 0)
    came = jnp.where(s == 2, cross, 0)
    lines = count - pre + came
    dma_to = functools.partial(pltpu.make_async_remote_copy, device_id_type=MESH)

    pl.semaphore_signal(ready.at[0], inc=1, device_id=(s, sib), device_id_type=MESH)

    @pl.when(z > 0)
    def _():
        pl.semaphore_signal(ready.at[2], inc=1, device_id=(s, d - 2), device_id_type=MESH)

    @pl.when(z < Z - 1)
    def _():
        pl.semaphore_signal(ready.at[1], inc=1, device_id=(s, d + 2), device_id_type=MESH)

    def small_copy(o):
        return dma_to(
            small_ref,
            small_in.at[d],
            small_send.at[o],
            small_recv.at[d],
            device_id=(s, lax.rem(d + o, ND)),
        )

    def small_wait(o):
        j = lax.rem(d + o, ND)
        return dma_to(
            small_ref, small_in.at[j], small_send.at[o], small_recv.at[j], device_id=(s, j)
        )

    for o in range(1, ND):
        small_copy(o).start()
    small_in[d] = small_ref[...]

    place_d = pl.ds(0, K)
    place_x = pl.ds((K + 127) // 128 * 128, K)
    for src, at_cols in ((dbr, place_d), (xin, place_x)):
        for i in range(D // 256):
            turned = flat(src, pl.ds(256 * i, 256)).T
            for q in range(8):
                t = 8 * i + q
                block = t * 32 // B
                at = block % 2 * R + block // 2 * B + t * 32 - block * B
                u[pl.ds(at, 32), at_cols] = turned[32 * q : 32 * q + 32]

    per = D // R

    def slot(j):
        return (pl.ds(pl.multiple_of(lax.rem(j, per) * R, 16), R), column(j // per, C))

    def slot_block(j, zt):
        r = pl.multiple_of(lax.rem(j, per) * R + zt * B, 16)
        return (pl.ds(r, B), column(j // per, C))

    def line_place(n, zt):
        r = pl.multiple_of(n // fold * R + zt * B, 16)
        return (pl.ds(r, B), column(lax.rem(n, fold), C))

    def cross_place(c):
        n = 2 * wide - cross + c
        r = pl.multiple_of(n // fold * R, 16)
        return (pl.ds(r, R), column(lax.rem(n, fold), C))

    def core_copy(j):
        return dma_to(
            core_out.at[lax.rem(j, 2)],
            w.at[slot(j)],
            core_send.at[lax.rem(j, 2)],
            core_recv.at[j],
            device_id=(s, sib),
        )

    def cross_copy(c):
        return dma_to(
            cross_out.at[c],
            ut.at[cross_place(c)],
            cross_send.at[c],
            cross_recv.at[c],
            device_id=(2, d),
        )

    def up_copy(n, zt):
        return dma_to(
            line_out.at[lax.rem(n, 2), zt],
            ut.at[line_place(n, zt)],
            line_send.at[lax.rem(n, 2), zt],
            up_recv.at[n, zt],
            device_id=(s, d + 2),
        )

    def down_copy(n, zt):
        return dma_to(
            line_out.at[lax.rem(n, 2), zt],
            wt.at[line_place(n, zt)],
            line_send.at[lax.rem(n, 2), zt],
            down_recv.at[n, zt],
            device_id=(s, d - 2),
        )

    def final_copy(n):
        j = n + pre
        early = j + cross * odd + (wide - own) * (1 - odd)
        at = jnp.where(j < first_kind, early, j - first_kind)
        return pltpu.make_async_copy(
            final.at[lax.rem(n, 2)], g_hbm.at[:, column(at, C)], final_sem.at[lax.rem(n, 2)]
        )

    def away(n):
        return ((s == 3) & (n < cross)) | ((s == 2) & (n >= count))

    def away_copy(n):
        c = n - jnp.where(s == 2, count, 0)
        return dma_to(
            final.at[lax.rem(n, 2)],
            g_hbm.at[:, column(wide + c, C)],
            away_send.at[lax.rem(n, 2)],
            away_recv.at[c],
            device_id=(jnp.where(s == 3, 2, 0), d),
        )

    def away_arrival(c):
        return dma_to(
            final.at[0],
            g_hbm.at[:, column(wide + c, C)],
            away_send.at[0],
            away_recv.at[c],
            device_id=(jnp.where(s == 3, 2, 0), d),
        )

    def final_wait(n):
        @pl.when(away(n))
        def _():
            away_copy(n).wait_send()

        @pl.when(jnp.logical_not(away(n)))
        def _():
            final_copy(n).wait()

    def total(n, zt):
        j = n + pre
        return keep[lax.rem(j, keeps), pl.ds(zt * B, B), :] + w[slot_block(j, zt)].astype(f32)

    near = jnp.minimum(z, Z - 1 - z)
    far = jnp.maximum(z, Z - 1 - z)

    def step(lo, hi, k, carry):
        @pl.when(k < count)
        def _():
            sl = lax.rem(k, 2)

            def products(place, right):
                @pl.when(k >= 2)
                def _():
                    core_copy(k - 2).wait_send()

                theirs = pl.ds(pl.multiple_of((1 - p) * R, 16), R)
                mine = pl.ds(pl.multiple_of(p * R, 16), R)
                core_out[sl] = dot(u[theirs, place], right).astype(bf16)

                @pl.when(k == 0)
                def _():
                    pl.semaphore_wait(ready.at[0], 1)

                core_copy(k).start()
                keep[lax.rem(k, keeps)] = dot(u[mine, place], right)

            @pl.when(k < first_kind)
            def _():
                products(place_d, flat(buf_a, column(k + (wide - own) * (1 - odd), C)))

            @pl.when(k >= first_kind)
            def _():
                products(place_x, flat(buf_b, column(k - first_kind, C)))

        @pl.when((lo >= count) & (k < count + came))
        def _():
            c = k - count
            cross_copy(c).wait_recv()
            keep[lax.rem(k, keeps)] = ut[cross_place(c)].astype(f32)
            w[slot(k)] = jnp.zeros((R, C), bf16)

        c_cross = k - 1

        @pl.when((c_cross >= 0) & (c_cross < pre))
        def _():
            core_copy(c_cross).wait_recv()
            both = keep[lax.rem(c_cross, keeps)] + w[slot(c_cross)].astype(f32)
            cross_out[c_cross] = both.astype(bf16)
            cross_copy(c_cross).start()

        n_near = k - 1 - pre - near

        @pl.when((n_near >= lo) & (n_near < hi) & (n_near + pre < count))
        def _():
            core_copy(n_near + pre).wait_recv()

        n_up = k - 1 - pre - z

        @pl.when((n_up >= lo) & (n_up < hi) & (z < Z - 1))
        def _():
            @pl.when(n_up == 0)
            def _():
                pl.semaphore_wait(ready.at[2], 1)

            for zt in range(Z - 1, 0, -1):
                @pl.when(zt > z)
                def _():
                    @pl.when(n_up >= 2)
                    def _():
                        up_copy(n_up - 2, zt).wait_send()

                    @pl.when(z > 0)
                    def _():
                        up_copy(n_up, zt).wait_recv()
                        line_out[lax.rem(n_up, 2), zt] = (
                            total(n_up, zt) + ut[line_place(n_up, zt)].astype(f32)
                        ).astype(bf16)

                    @pl.when(z == 0)
                    def _():
                        line_out[lax.rem(n_up, 2), zt] = total(n_up, zt).astype(bf16)

                    up_copy(n_up, zt).start()

        n_down = k - 1 - pre - (Z - 1 - z)

        @pl.when((n_down >= lo) & (n_down < hi) & (z > 0))
        def _():
            @pl.when(n_down == 0)
            def _():
                pl.semaphore_wait(ready.at[1], 1)

            for zt in range(Z - 1):
                @pl.when(zt < z)
                def _():
                    @pl.when(n_down >= 2)
                    def _():
                        down_copy(n_down - 2, zt).wait_send()

                    @pl.when(z < Z - 1)
                    def _():
                        down_copy(n_down, zt).wait_recv()
                        line_out[lax.rem(n_down, 2), zt] = (
                            total(n_down, zt) + wt[line_place(n_down, zt)].astype(f32)
                        ).astype(bf16)

                    @pl.when(z == Z - 1)
                    def _():
                        line_out[lax.rem(n_down, 2), zt] = total(n_down, zt).astype(bf16)

                    down_copy(n_down, zt).start()

        n_own = k - 1 - pre - far

        @pl.when((n_own >= lo) & (n_own < hi))
        def _():
            sl = lax.rem(n_own, 2)

            @pl.when(n_own >= 2)
            def _():
                final_wait(n_own - 2)

            final[sl] = total(n_own, z)

            @pl.when(z > 0)
            def _():
                up_copy(n_own, z).wait_recv()
                final[sl] += ut[line_place(n_own, z)].astype(f32)

            @pl.when(z < Z - 1)
            def _():
                down_copy(n_own, z).wait_recv()
                final[sl] += wt[line_place(n_own, z)].astype(f32)

            @pl.when(away(n_own))
            def _():
                away_copy(n_own).start()

            @pl.when(jnp.logical_not(away(n_own)))
            def _():
                final_copy(n_own).start()

        return carry

    own_lines = count - pre
    lax.fori_loop(0, count + 1 + far, functools.partial(step, 0, own_lines), 0)
    later = jnp.where(s == 2, count + came + 1 + far, count)
    lax.fori_loop(count, later, functools.partial(step, count, count + came), 0)

    for back in (2, 1):
        core_copy(count - back).wait_send()
        n = lines - back
        for zt in range(Z):
            @pl.when(zt > z)
            def _():
                up_copy(n, zt).wait_send()

            @pl.when(zt < z)
            def _():
                down_copy(n, zt).wait_send()

        final_wait(n)

    @pl.when(s == 1)
    def _():
        for c in range(cross):
            cross_copy(c).wait_send()

    @pl.when(odd == 0)
    def _():
        for c in range(cross):
            away_arrival(c).wait_recv()

    for o in range(1, ND):
        small_wait(o).wait_recv()
        small_copy(o).wait_send()
    acc = small_in[0]
    for j in range(1, ND):
        acc = acc + small_in[j]
    small_ref[...] = acc
    bias_out, gain_out, shift_out = small_outs
    P = FF // ND
    bias_out[...] = small_ref[:, pl.ds(pl.multiple_of(d * P, 128), P)]
    for j in range(ND):
        @pl.when(d == j)
        def _():
            gain_out[...] = acc[:, FF + B * j : FF + B * j + B]
            shift_out[...] = acc[:, FF + D + B * j : FF + D + B * j + B]


def pipeline_kernel(
    cfg,
    len_ref,
    x_hbm,
    cot_hbm,
    pred_ref,
    slab_hbm,
    bias_ref,
    gain_ref,
    shift_ref,
    draws_ref,
    out_hbm,
    grad_hbm,
    g_hbm,
    *refs,
):
    M, L, LP, D, FF, HD, FE, NS, ND, fscale, in_kernel, C = cfg
    small_outs = refs[:3] if in_kernel else ()
    small_ref = refs[3] if in_kernel else refs[0]
    fmap_ref = refs[4] if in_kernel else refs[1]
    (
        w,
        u,
        wt,
        ut,
        xin,
        out,
        dyin,
        dxo,
        dbr,
        nbuf,
        rbuf,
        buf_a,
        buf_b,
        land,
        out_stage,
        grad_stage,
        load_sem,
        x_sem,
        u_send,
        u_recv,
        f_send,
        f_recv,
        b_send,
        b_recv,
        stage_sem,
        g_sem,
        *reduce_refs,
    ) = refs[5:] if in_kernel else refs[2:]
    HALF = FF // 2
    GH = 256 // HD
    G = D // 256
    GF = GH * FE
    top = (LP // 2 + 15) // 16 * 16
    halves = (pl.ds(0, top), pl.ds(top, LP - top))
    whole = pl.ds(0, LP)
    relay_lo, relay_hi = RELAYED if NS == 4 else (0, 0)
    relayed = relay_hi - relay_lo
    s = lax.axis_index("section")
    d = lax.axis_index("dp")
    odd = lax.rem(s, 2)
    is_attn = odd == 0
    is_ff = odd == 1
    first = s == 0
    last = s == NS - 1
    sib = d + 1 - 2 * lax.rem(d, 2)
    mate = d + 2 - 4 * lax.rem(d // 2, 2)
    quarter = D // 4
    pieces = 4
    piece = quarter // pieces

    barrier = pltpu.get_barrier_semaphore()

    def greet(cond, ts, td):
        @pl.when(cond)
        def _():
            pl.semaphore_signal(barrier, inc=1, device_id=(ts, td), device_id_type=MESH)

    always = s >= 0
    partners = 2
    if in_kernel:
        partners = ND - 1
        for o in range(1, ND):
            greet(always, s, lax.rem(d + o, ND))
    else:
        greet(always, s, sib)
        greet(always, s, mate)
    greet(s > 0, s - 1, d)
    greet(s < NS - 1, s + 1, d)
    if relayed > 0 or in_kernel:
        greet(s == 0, 2, d)
        greet(s == 2, 0, d)
        extra = jnp.where(lax.rem(s, 2) == 0, 1, 0)
    else:
        extra = 0

    w_copy = pltpu.make_async_copy(slab_hbm.at[0, :, pl.ds(0, FF)], w, load_sem.at[0])
    u_copy = pltpu.make_async_copy(
        slab_hbm.at[0, :, pl.ds(FF, HALF)], u.at[:, pl.ds(HALF, HALF)], load_sem.at[1]
    )
    w_copy.start()

    def land_copy(ref, m):
        sl = lax.rem(m, 2)
        return pltpu.make_async_copy(ref.at[m], land.at[sl], x_sem.at[sl])

    @pl.when(first)
    def _():
        for m in range(2):
            land_copy(x_hbm, m).start()

    @pl.when(last)
    def _():
        for m in range(2):
            land_copy(cot_hbm, m).start()

    @pl.when(is_ff)
    def _():
        u_copy.start()

    small_ref[...] = jnp.zeros_like(small_ref)
    bias_grad_ref = small_ref.at[:, pl.ds(0, FF)]
    gain_grad_ref = small_ref.at[:, pl.ds(FF, D)]
    shift_grad_ref = small_ref.at[:, pl.ds(FF + D, D)]

    @pl.when(first | last)
    def _():
        pl.semaphore_wait(barrier, partners + 1 + extra)

    @pl.when((s > 0) & (s < NS - 1))
    def _():
        pl.semaphore_wait(barrier, partners + 2 + extra)

    q0 = lax.rem(d, 4)
    q1 = q0 + 2 - 4 * (q0 // 2)
    left = pl.ds(0, HALF)

    def u_rows(q, i):
        return pl.ds(pl.multiple_of(q * quarter + i * piece, piece), piece)

    def u_from_section(i):
        return pltpu.make_async_remote_copy(
            slab_hbm.at[0, u_rows(q0, i), pl.ds(FF, HALF)],
            u.at[u_rows(q0, i), left],
            u_send.at[0, i],
            u_recv.at[0, i],
            device_id=(s + 1, d),
            device_id_type=MESH,
        )

    def u_copy_to(q, i, k, to):
        return pltpu.make_async_remote_copy(
            u.at[u_rows(q, i), left],
            u.at[u_rows(q, i), left],
            u_send.at[k, i],
            u_recv.at[k, i],
            device_id=(s, to),
            device_id_type=MESH,
        )

    @pl.when(is_attn & (s < NS - 1))
    def _():
        for i in range(pieces):
            u_from_section(i).start()

    def turn(src, dst, start, count):
        for i in range(start, start + count):
            dst[pl.ds(256 * i, 256), :] = src[:, pl.ds(256 * i, 256)].T

    w_copy.wait()
    late_turn = first

    @pl.when(is_attn)
    def _():
        turn(w, wt, 3 * D // 256, D // 256)
        f_row = lax.broadcasted_iota(jnp.int32, (FE, GF), 0)
        f_col = lax.broadcasted_iota(jnp.int32, (FE, GF), 1)
        for n in range(G * GH):
            shift = jnp.where(f_col == f_row + n % GH * FE, 1.0, 0.0).astype(bf16)
            spread = dot(draws_ref[n].astype(f32).astype(bf16), shift)
            fmap_ref[n // GH, pl.ds(n % GH * HD, HD), :] = spread.astype(bf16)

    @pl.when(s == 2)
    def _():
        turn(w, wt, 0, 3 * D // 256)

    @pl.when(is_ff)
    def _():
        turn(w, wt, 0, FF // 256)
        u_copy.wait()
        turn(u, ut, HALF // 256, HALF // 256)
        for i in range(pieces):
            u_from_section(i).wait_recv()
            u_copy_to(q0, i, 1, mate).start()
            u_copy_to(q0, i, 2, sib).start()
            if i > 0:
                u_copy_to(q0, i - 1, 1, mate).wait_recv()
                u_copy_to(q1, i - 1, 3, sib).start()
        u_copy_to(q0, pieces - 1, 1, mate).wait_recv()
        u_copy_to(q1, pieces - 1, 3, sib).start()
        for i in range(pieces):
            u_copy_to(q0, i, 2, sib).wait_recv()
            u_copy_to(q1, i, 3, sib).wait_recv()
        turn(u, ut, 0, HALF // 256)

    g_row = gain_ref[...]
    b_row = shift_ref[...]
    head_mask = block_mask(GF, 256, FE, HD)
    pair_mask = jnp.concatenate([head_mask, head_mask], axis=1)

    def sz_at(m, g):
        n = m * G + g
        r = pl.multiple_of(lax.rem(n, D // GF) * GF, GF)
        c = pl.multiple_of(n // (D // GF) * 512, 512)
        return (pl.ds(r, GF), pl.ds(c, 512))

    def valid_rows(m, rows):
        at = lax.broadcasted_iota(jnp.int32, (rows.size, GF), 0) + rows.start
        return at < len_ref[m]

    def with_ones(v):
        return jnp.concatenate([v, jnp.ones(v.shape, bf16)], axis=1)

    def norm_forward(m, rows, pre):
        mean = jnp.mean(pre, axis=-1, keepdims=True)
        cen = pre - mean
        r = lax.rsqrt(jnp.mean(cen * cen, axis=-1, keepdims=True) + norm_epsilon)
        n = cen * r
        nbuf[m, rows, :] = n
        rbuf[m, rows, :] = r
        out[m, rows, :] = (n * g_row + b_row).astype(bf16)

    def norm_backward(m, rows):
        dy = dyin[m, rows, :].astype(f32)
        n = nbuf[m, rows, :]
        dn = dy * g_row
        m1 = jnp.mean(dn, axis=-1, keepdims=True)
        m2 = jnp.mean(dn * n, axis=-1, keepdims=True)
        gain_grad_ref[...] += jnp.sum(dy * n, axis=0, keepdims=True)
        shift_grad_ref[...] += jnp.sum(dy, axis=0, keepdims=True)
        dpre = rbuf[m, rows, :] * (dn - m1 - n * m2)
        dbr[m, rows, :] = dpre.astype(bf16)
        return dpre

    def next_copy(m, h):
        return pltpu.make_async_remote_copy(
            out.at[m, halves[h]],
            xin.at[m, halves[h]],
            f_send.at[m, h],
            f_recv.at[m, h],
            device_id=(s + 1, d),
            device_id_type=MESH,
        )

    def back_copy(m, h):
        return pltpu.make_async_remote_copy(
            dxo.at[m, halves[h]],
            dyin.at[m, halves[h]],
            b_send.at[m, h],
            b_recv.at[m, h],
            device_id=(s - 1, d),
            device_id_type=MESH,
        )

    def relay_at(m, h):
        start = pl.multiple_of(m * LP + halves[h].start, 16)
        return ut.at[pl.ds(start, halves[h].size)]

    def relay_in(m, h):
        return pltpu.make_async_remote_copy(
            dxo.at[m, halves[h]],
            relay_at(m, h),
            b_send.at[m, h],
            f_recv.at[m, h],
            device_id=(0, d),
            device_id_type=MESH,
        )

    def relay_on(m, h):
        return pltpu.make_async_remote_copy(
            relay_at(m, h),
            dyin.at[m, halves[h]],
            b_send.at[m, h],
            b_recv.at[m, h],
            device_id=(1, d),
            device_id_type=MESH,
        )

    def send_next(m, h):
        if h == 0:
            @pl.when(is_attn & (m == 0))
            def _():
                for i in range(pieces):
                    u_from_section(i).wait_send()

        @pl.when(s < NS - 1)
        def _():
            next_copy(m, h).start()

    def by_relay(m):
        return (s == 2) & (m >= relay_lo) & (m < relay_hi)

    def send_back(m, h):
        @pl.when((s > 0) & jnp.logical_not(by_relay(m)))
        def _():
            back_copy(m, h).start()

        @pl.when(by_relay(m))
        def _():
            relay_in(m, h).start()

    v_at = [pl.ds(256 * g, 256) for g in range(G)]
    fq_at = [pl.ds(D + GF * g, GF) for g in range(G)]
    fk_at = [pl.ds(D + GF * (G + g), GF) for g in range(G)]
    out_at = pl.ds(3 * D, D)

    def attend_features(m, rows):
        x = xin[m, rows, :]
        valid = valid_rows(m, rows)
        for g in range(G):
            qkv = [
                (dot(x, w[:, c]) + bias_ref[:, c]).astype(bf16)
                for c in (pl.ds(k * D + 256 * g, 256) for k in range(3))
            ]
            fq = softplus(dot(qkv[0], fmap_ref[g]) * fscale).astype(bf16)
            fk = softplus(dot(qkv[1], fmap_ref[g]) * fscale)
            buf_a[m, rows, v_at[g]] = qkv[2]
            buf_a[m, rows, fq_at[g]] = fq
            buf_a[m, rows, fk_at[g]] = jnp.where(valid, fk, 0.0).astype(bf16)

    def summaries(m):
        for g in range(G):
            sz = dot_rows(buf_a[m, :, fk_at[g]], with_ones(buf_a[m, :, v_at[g]]))
            u[sz_at(m, g)] = jnp.where(pair_mask, sz, 0.0).astype(bf16)

    def attend_mix(m, rows):
        for g in range(G):
            nd = dot(buf_a[m, rows, fq_at[g]], u[sz_at(m, g)])
            mixed = (nd[:, :256] / nd[:, 256:]).astype(bf16)
            buf_a[m, rows, pl.ds(3 * D + 256 * g, 256)] = mixed
        branch = dot(buf_a[m, rows, out_at], wt[out_at, :]) + bias_ref[:, out_at]
        norm_forward(m, rows, xin[m, rows, :].astype(f32) + branch)

    def attend_forward(m, mode):
        if mode == 2:
            attend_features(m, whole)
            summaries(m)
            attend_mix(m, whole)
            send_next(m, 0)
            send_next(m, 1)
            return
        attend_features(m, halves[mode])
        if mode == 1:
            summaries(m)
            for part, rows in enumerate(halves):
                attend_mix(m, rows)
                send_next(m, part)

    def feed_forward(m, mode):
        rows = (halves + (whole,))[mode]
        x = xin[m, rows, :]
        tile = 512
        for j in range(FF // tile):
            c = pl.ds(j * tile, tile)
            a = dot(x, w[:, c]) + bias_ref[:, c]
            cdf = 0.5 + 0.5 * lax.erf(a * 0.7071067811865476)
            pdf = jnp.exp(a * a * -0.5) * 0.3989422804014327
            buf_a[m, rows, c] = (a * cdf).astype(bf16)
            buf_b[m, rows, c] = (cdf + a * pdf).astype(bf16)
        branch = dot(buf_a[m, rows, :], ut[...])
        norm_forward(m, rows, x.astype(f32) + branch)
        for h in (mode,) if mode < 2 else (0, 1):
            send_next(m, h)

    def attend_backward(m, mode):
        rows = (halves + (whole,))[mode]
        dpre = norm_backward(m, rows)
        nbuf[m, rows, :] = dpre
        db = dbr[m, rows, :]
        bias_grad_ref[:, out_at] += jnp.sum(db.astype(f32), axis=0, keepdims=True)

        def store(rows, k, g, val):
            c = pl.ds(k * D + 256 * g, 256)
            buf_b[m, rows, c] = val
            bias_grad_ref[:, c] += jnp.sum(val.astype(f32), axis=0, keepdims=True)

        for g in range(G):
            dmix = dot(db, w[:, pl.ds(3 * D + 256 * g, 256)])
            fq = buf_a[m, rows, fq_at[g]]
            sz = u[sz_at(m, g)]
            nd = dot(fq, sz)
            rden = 1.0 / nd[:, 256:]
            dnum = dmix * rden
            dden = -dnum * (nd[:, :256] * rden)
            de = jnp.concatenate([dnum, dden], axis=1).astype(bf16)
            buf_b[m, rows, pl.ds(D + 512 * g, 512)] = de
            duq = dot_cols(de, sz) * (1.0 - jnp.exp(-fq.astype(f32)))
            dq = (dot_cols(duq.astype(bf16), fmap_ref[g]) * fscale).astype(bf16)
            store(rows, 0, g, dq)
        if mode == 0:
            return
        for g in range(G):
            dsz = dot_rows(buf_a[m, :, fq_at[g]], buf_b[m, :, pl.ds(D + 512 * g, 512)])
            u[sz_at(m, g)] = jnp.where(pair_mask, dsz, 0.0).astype(bf16)
        for part, rows in enumerate(halves if mode == 1 else (whole,)):
            valid = valid_rows(m, rows)
            for g in range(G):
                dsz = u[sz_at(m, g)]
                fk = buf_a[m, rows, fk_at[g]]
                dfk = dot_cols(with_ones(buf_a[m, rows, v_at[g]]), dsz)
                duk = jnp.where(valid, dfk, 0.0) * (1.0 - jnp.exp(-fk.astype(f32)))
                dk = (dot_cols(duk.astype(bf16), fmap_ref[g]) * fscale).astype(bf16)
                store(rows, 1, g, dk)
                store(rows, 2, g, dot(fk, dsz[:, :256]).astype(bf16))
            inner = pl.ds(0, 3 * D)
            dx = nbuf[m, rows, :] + dot(buf_b[m, rows, inner], wt[inner, :])
            dxo[m, rows, :] = dx.astype(bf16)
            for h in (part,) if mode == 1 else (0, 1):
                send_back(m, h)

    def feed_backward(m, mode):
        rows = (halves + (whole,))[mode]
        dpre = norm_backward(m, rows)
        db = dbr[m, rows, :]
        tile = 512
        for j in range(FF // tile):
            c = pl.ds(j * tile, tile)
            da = (dot(db, u[:, c]) * buf_b[m, rows, c].astype(f32)).astype(bf16)
            buf_b[m, rows, c] = da
            bias_grad_ref[:, c] += jnp.sum(da.astype(f32), axis=0, keepdims=True)
        dx = dpre + dot(buf_b[m, rows, :], wt[...])
        dxo[m, rows, :] = dx.astype(bf16)
        for h in (mode,) if mode < 2 else (0, 1):
            send_back(m, h)

    def out_copy(m):
        return pltpu.make_async_copy(out_stage, out_hbm.at[m], stage_sem.at[0])

    def grad_copy(m):
        return pltpu.make_async_copy(grad_stage, grad_hbm.at[m], stage_sem.at[1])

    def write_out(copy, rows, staged, m):
        @pl.when(m >= 1)
        def _():
            copy(m - 1).wait()

        staged[...] = rows[m, pl.ds(0, L), :]
        copy(m).start()

    pad_zero = jnp.zeros((LP - L, D), bf16)
    eye = lax.broadcasted_iota(jnp.int32, (L, L), 0) == lax.broadcasted_iota(jnp.int32, (L, L), 1)

    def forward_step(m, mode):
        if mode != 1:
            @pl.when(first)
            def _():
                land_copy(x_hbm, m).wait()
                xin[m] = jnp.concatenate([land[lax.rem(m, 2)], pad_zero], axis=0)

                @pl.when(m + 2 < M)
                def _():
                    land_copy(x_hbm, m + 2).start()

        @pl.when(s > 0)
        def _():
            for h in (mode,) if mode < 2 else (0, 1):
                next_copy(m, h).wait_recv()

        @pl.when(is_attn)
        def _():
            attend_forward(m, mode)

        @pl.when(is_ff)
        def _():
            feed_forward(m, mode)

        if mode > 0:
            write_out(out_copy, out, out_stage, m)
        if mode == 1:
            @pl.when(first & (m == M - 1))
            def _():
                turn(w, wt, 0, 3 * D // 256)

    def backward_step(m, mode):
        if mode != 1:
            @pl.when(last)
            def _():
                land_copy(cot_hbm, m).wait()
                row = jnp.where(
                    lax.broadcasted_iota(jnp.int32, (1, L), 1) < len_ref[m],
                    pred_ref[pl.ds(m, 1), :].astype(f32),
                    0.0,
                )
                col = jnp.sum(jnp.where(eye, row, 0.0), axis=1, keepdims=True)
                masked = (land[lax.rem(m, 2)].astype(f32) * col).astype(bf16)
                dyin[m] = jnp.concatenate([masked, pad_zero], axis=0)

                @pl.when(m + 2 < M)
                def _():
                    land_copy(cot_hbm, m + 2).start()

        @pl.when(s < NS - 1)
        def _():
            for h in (mode,) if mode < 2 else (0, 1):
                back_copy(m, h).wait_recv()

        @pl.when(is_attn)
        def _():
            attend_backward(m, mode)

        @pl.when(is_ff)
        def _():
            feed_backward(m, mode)

        if mode > 0:
            write_out(grad_copy, dxo, grad_stage, m)

    back_start = jnp.where(s == 0, 16, jnp.where(s == 1, 12, jnp.where(s == 2, 10, 6)))
    relay_start = 12

    def when_due(start, act):
        def at(t):
            i = t - start
            m = i // 2

            apart = i < 0
            for n in SPLIT:
                apart = apart | (m == n % M)
            here = (i >= 0) & (i < 2 * M)

            @pl.when(here & jnp.logical_not(apart) & (lax.rem(i, 2) == 1))
            def _():
                act(m, 2)

            for h in range(2):
                @pl.when(here & apart & (lax.rem(i, 2) == h))
                def _():
                    act(m, h)

        return at

    forward_at = when_due(2 * s, forward_step)
    backward_at = when_due(back_start, backward_step)

    def tick(t, carry):
        forward_at(t)
        if relayed > 0:
            i = t - relay_start
            for h in range(2):
                @pl.when((s == 0) & (i >= 0) & (i < 2 * relayed) & (lax.rem(i, 2) == h))
                def _():
                    relay_in(relay_lo + i // 2, h).wait_recv()
                    relay_on(relay_lo + i // 2, h).start()
        backward_at(t)
        return carry

    lax.fori_loop(0, 28, tick, 0)

    if relayed > 0:
        @pl.when(s == 0)
        def _():
            for m in range(relay_lo, relay_hi):
                for h in range(2):
                    relay_on(m, h).wait_send()

    @pl.when(is_ff)
    def _():
        for i in range(pieces):
            u_copy_to(q0, i, 1, mate).wait_send()
            u_copy_to(q0, i, 2, sib).wait_send()
            u_copy_to(q1, i, 3, sib).wait_send()

    if in_kernel:
        reduce_gradients(
            cfg,
            s,
            d,
            odd,
            w,
            u,
            wt,
            ut,
            xin,
            dbr,
            buf_a,
            buf_b,
            g_hbm,
            small_ref,
            small_outs,
            *reduce_refs,
        )
    else:
        plain_gradients(cfg, odd, xin, dbr, buf_a, buf_b, g_hbm, g_sem, *reduce_refs)

    for m in range(M):
        for h in range(2):
            @pl.when(s < NS - 1)
            def _():
                next_copy(m, h).wait_send()

            @pl.when(s > 0)
            def _():
                back_copy(m, h).wait_send()

    out_copy(M - 1).wait()
    grad_copy(M - 1).wait()


def shards(
    block_input, cotangent, lengths, predicted, slab, in_bias, norm_gain, norm_bias, feature_draws
):
    NS = lax.axis_size("section")
    ND = lax.axis_size("dp")
    M, L, D = block_input.shape
    FF = in_bias.shape[1]
    H, HD, FE = feature_draws.shape
    LP = (L + 15) // 16 * 16
    GH = 256 // HD
    G = D // 256
    GF = GH * FE
    fscale = float((3.0 / (20.0 * HD)) ** 0.5)
    in_kernel = D // ND % 32 == 0 and NS == 4
    C = CHUNK if in_kernel else D
    cfg = (M, L, LP, D, FF, HD, FE, NS, ND, fscale, in_kernel, C)
    hbm = pl.BlockSpec(memory_space=pl.ANY)
    vmem = pl.BlockSpec(memory_space=pltpu.VMEM)
    smem = pl.BlockSpec(memory_space=pltpu.SMEM)
    dma = pltpu.SemaphoreType.DMA
    rows_bf = pltpu.VMEM((M, LP, D), bf16)
    wide_bf = pltpu.VMEM((M, LP, FF), bf16)
    small_size = FF + 2 * D
    smalls = [FF // ND, D // ND, D // ND] if in_kernel else [small_size]
    scratch = [pltpu.VMEM((1, small_size), f32)] if in_kernel else []
    scratch += [
        pltpu.VMEM((G, GH * HD, GF), bf16),
        pltpu.VMEM((D, FF), bf16),
        pltpu.VMEM((D, FF), bf16),
        pltpu.VMEM((FF, D), bf16),
        pltpu.VMEM((FF, D), bf16),
        rows_bf,
        rows_bf,
        rows_bf,
        rows_bf,
        rows_bf,
        pltpu.VMEM((M, LP, D), f32),
        pltpu.VMEM((M, LP, 1), f32),
        wide_bf,
        wide_bf,
        pltpu.VMEM((2, L, D), bf16),
        pltpu.VMEM((L, D), bf16),
        pltpu.VMEM((L, D), bf16),
        dma((2,)),
        dma((2,)),
        dma((4, 4)),
        dma((4, 4)),
        dma((M, 2)),
        dma((M, 2)),
        dma((M, 2)),
        dma((M, 2)),
        dma((2,)),
        dma((1,)),
    ]
    if in_kernel:
        Z, B, chunks = ND // 2, D // ND, 2 * FF // C
        cross = FF // C // 2
        lines = chunks
        scratch += [
            pltpu.SemaphoreType.REGULAR((3,)),
            pltpu.VMEM((Z + 1, Z * B, C), f32),
            pltpu.VMEM((2, Z * B, C), bf16),
            pltpu.VMEM((cross, Z * B, C), bf16),
            pltpu.VMEM((2, Z, B, C), bf16),
            pltpu.VMEM((2, B, C), f32),
            pltpu.VMEM((ND, 1, small_size), f32),
            dma((2,)),
            dma((chunks,)),
            dma((2, Z)),
            dma((lines, Z)),
            dma((lines, Z)),
            dma((2,)),
            dma((cross,)),
            dma((cross,)),
            dma((cross,)),
            dma((cross,)),
            dma((ND,)),
            dma((ND,)),
        ]
        g_shape = (B, FF + FF // 2)
    else:
        scratch += [pltpu.VMEM((D, D), f32)]
        g_shape = (D, 2 * FF)
    section_out, section_grad, grads, *small = pl.pallas_call(
        functools.partial(pipeline_kernel, cfg),
        out_shape=[
            jax.ShapeDtypeStruct((M, L, D), bf16),
            jax.ShapeDtypeStruct((M, L, D), bf16),
            jax.ShapeDtypeStruct(g_shape, f32),
        ]
        + [jax.ShapeDtypeStruct((1, n), f32) for n in smalls],
        in_specs=[smem, hbm, hbm, vmem, hbm, vmem, vmem, vmem, vmem],
        out_specs=[hbm, hbm, hbm] + [vmem] * len(smalls),
        scratch_shapes=scratch,
        compiler_params=pltpu.CompilerParams(
            collective_id=0, has_side_effects=True, vmem_limit_bytes=62 * 2**20
        ),
        name="pipeline",
    )(
        lengths,
        block_input,
        cotangent,
        predicted,
        slab,
        in_bias,
        norm_gain,
        norm_bias,
        feature_draws,
    )
    if in_kernel:
        own = grads
        parts = small
    else:
        def scatter(value):
            return lax.psum_scatter(value, "dp", scatter_dimension=0, tiled=True)

        HALF = FF // 2
        both = scatter(grads)
        sums = small[0][0]
        parts = [scatter(v)[None] for v in (sums[:FF], sums[FF : FF + D], sums[FF + D :])]
        is_attention = lax.axis_index("section") % 2 == 0
        turned = jnp.where(
            is_attention,
            jnp.concatenate([both[:, D:FF], both[:, :D], both[:, FF:]], axis=1),
            jnp.concatenate([both[:, FF:], both[:, :FF]], axis=1),
        )
        pairs = [(i, i - 1) for i in range(1, NS, 2)]
        arrived = lax.ppermute(turned[:, FF : FF + HALF], "section", pairs)
        rest = jnp.where(is_attention, arrived, turned[:, FF + HALF :])
        own = jnp.concatenate([turned[:, :FF], rest], axis=1)
    return (
        section_out[None],
        section_grad[None],
        own[None],
        *parts,
    )


def solution(mesh):
    placed = (
        P("dp", None, None),
        P("dp", None, None),
        P("dp"),
        P("dp", None),
        P("section", None, None),
        P("section", None),
        P("section", None),
        P("section", None),
        P(),
    )
    return jax.shard_map(
        shards,
        mesh=mesh,
        in_specs=placed,
        out_specs=(
            P("section", "dp", None, None),
            P("section", "dp", None, None),
            P("section", "dp", None),
            P("section", "dp"),
            P("section", "dp"),
            P("section", "dp"),
        ),
        check_vma=False,
    )
```

profile of v0, /device:TPU:2, one launch (start us, length us, event | category | flops | bytes accessed | tf_op | source)
XLA Modules:
  0.0 200.0 jit_solution(15962011791893059628)
XLA Ops:
  0.6 1.8 copy.15.draws_ref
  2.5 189.4 %pipeline.1 = (bf16[6,202,768]{2,1,0:T(8,128)(2,1)}, bf16[6,202,768]{2,1,0:T(8,128)(2,1)}, f32[96,4608]{1,0:T(8,128)}, f32[1,384]{1,0:T(1,128)}, f32[1,96]{1,0:T(1,128)}, /*index=5*/f32[1,96]{1,0:T(1,128)}) custom-call(s32[6]{0:T(128)} %len_ref.1, bf16[6,202,768]{2,1,0:T(8,128)(2,1)} %x_hbm.1, bf16[6,202,768]{2,1,0:T(8,128)(2,1)} %cot_hbm.1, ...), custom_call_target="tpu_custom_call" | custom-call | tf_op jit(solution)/shard_map/pipeline/pallas_call | solution.py:1164
  191.9 0.0 copy-start
  191.9 3.0 %copy.22 = bf16[1,6,202,768]{3,2,1,0:T(8,128)(2,1)} copy(bf16[1,6,202,768]{3,2,1,0:T(8,128)(2,1)} %bitcast.4) | data formatting | bytes 3723264
  195.0 0.0 copy-done
  195.0 0.0 copy-start.1
  195.0 1.3 copy.23
  196.2 0.9 copy-done.1
  197.2 0.0 copy-start.2
  197.2 0.0 copy-start.4
  197.2 0.0 copy-start.3
  197.2 1.2 copy.24
  198.4 0.0 copy-done.2
  198.4 0.6 copy.25
  198.9 0.0 copy-done.4
  198.9 0.5 copy.26
  199.4 0.0 copy-done.3
  199.5 0.5 copy.27
Async XLA Ops:
  191.9 3.1 %copy-start = (bf16[6,202,768]{2,1,0:T(8,128)(2,1)S(1)}, bf16[6,202,768]{2,1,0:T(8,128)(2,1)}, u32[]{:S(2)}) copy-start(bf16[6,202,768]{2,1,0:T(8,128)(2,1)} %get-tuple-element.13) | copy-start | bytes 5584900
  195.0 2.2 %copy-start.1 = (f32[96,4608]{1,0:T(8,128)S(1)}, f32[96,4608]{1,0:T(8,128)}, u32[]{:S(2)}) copy-start(f32[96,4608]{1,0:T(8,128)} %get-tuple-element.14) | copy-start | bytes 5308420
  197.2 1.2 copy-start.2
  197.2 1.8 copy-start.4
  197.2 2.3 %copy-start.3 = (f32[1,96]{1,0:T(1,128)S(1)}, f32[1,96]{1,0:T(1,128)}, u32[]{:S(2)}) copy-start(f32[1,96]{1,0:T(1,128)} %get-tuple-element.29) | copy-start | bytes 1156
where the time goes:
time: 200 us
  Pallas kernels  189 us (94%)
  local copies, waits for them, and re-layouts  9.87 us (5%)
    pallas_call x1, Pallas kernels, shards(): pl.pallas_call(functools.partial(pipeline_kernel, cfg), out_shape=[jax.Sh...  189 us
    unnamed x17, local copies, waits for them, and re-layouts  9.87 us

commit v1 on v0

--- a/solution.py
+++ b/solution.py
@@ -10,7 +10,7 @@
 MESH = pl.DeviceIdType.MESH
 CHUNK = 384
 RELAYED = (0, 3)
-SPLIT = (-1, -1)
+SPLIT = ()
 norm_epsilon = 1e-05
 bf16 = jnp.bfloat16
 f32 = jnp.float32
@@ -140,8 +140,9 @@
     sib = d + 1 - 2 * p
     first_kind, count = chunk_counts(cfg, odd)
     cross = wide // 2
-    pre = jnp.where(s == 1, cross, 0)
-    came = jnp.where(s == 2, cross, 0)
+    shipped = cross + 1
+    pre = jnp.where(s == 1, shipped, 0)
+    came = jnp.where(s == 2, shipped, 0)
     lines = count - pre + came
     dma_to = functools.partial(pltpu.make_async_remote_copy, device_id_type=MESH)
 
@@ -203,6 +204,8 @@
         r = pl.multiple_of(n // fold * R, 16)
         return (pl.ds(r, R), column(lax.rem(n, fold), C))
 
+    spare = (pl.ds(0, R), pl.ds(FF - (C + 127) // 128 * 128, C))
+
     def core_copy(j):
         return dma_to(
             core_out.at[lax.rem(j, 2)],
@@ -221,6 +224,15 @@
             device_id=(2, d),
         )
 
+    def spare_copy():
+        return dma_to(
+            cross_out.at[cross],
+            u.at[spare],
+            cross_send.at[cross],
+            cross_recv.at[cross],
+            device_id=(2, d),
+        )
+
     def up_copy(n, zt):
         return dma_to(
             line_out.at[lax.rem(n, 2), zt],
@@ -252,18 +264,19 @@
 
     def away_copy(n):
         c = n - jnp.where(s == 2, count, 0)
+        to = jnp.where(s == 3, 2, c // cross)
         return dma_to(
             final.at[lax.rem(n, 2)],
-            g_hbm.at[:, column(wide + c, C)],
+            g_hbm.at[:, column(wide + lax.rem(c, cross), C)],
             away_send.at[lax.rem(n, 2)],
             away_recv.at[c],
-            device_id=(jnp.where(s == 3, 2, 0), d),
+            device_id=(to, d),
         )
 
     def away_arrival(c):
         return dma_to(
             final.at[0],
-            g_hbm.at[:, column(wide + c, C)],
+            g_hbm.at[:, column(wide + c % cross, C)],
             away_send.at[0],
             away_recv.at[c],
             device_id=(jnp.where(s == 3, 2, 0), d),
@@ -285,56 +298,81 @@
     near = jnp.minimum(z, Z - 1 - z)
     far = jnp.maximum(z, Z - 1 - z)
 
-    def step(lo, hi, k, carry):
-        @pl.when(k < count)
-        def _():
-            sl = lax.rem(k, 2)
-
-            def products(place, right):
-                @pl.when(k >= 2)
-                def _():
-                    core_copy(k - 2).wait_send()
-
-                theirs = pl.ds(pl.multiple_of((1 - p) * R, 16), R)
-                mine = pl.ds(pl.multiple_of(p * R, 16), R)
-                core_out[sl] = dot(u[theirs, place], right).astype(bf16)
-
-                @pl.when(k == 0)
-                def _():
-                    pl.semaphore_wait(ready.at[0], 1)
-
-                core_copy(k).start()
-                keep[lax.rem(k, keeps)] = dot(u[mine, place], right)
-
-            @pl.when(k < first_kind)
-            def _():
-                products(place_d, flat(buf_a, column(k + (wide - own) * (1 - odd), C)))
-
-            @pl.when(k >= first_kind)
-            def _():
-                products(place_x, flat(buf_b, column(k - first_kind, C)))
-
-        @pl.when((lo >= count) & (k < count + came))
-        def _():
-            c = k - count
+    def make(k):
+        sl = lax.rem(k, 2)
+
+        def products(place, right):
+            @pl.when(k >= 2)
+            def _():
+                core_copy(k - 2).wait_send()
+
+            theirs = pl.ds(pl.multiple_of((1 - p) * R, 16), R)
+            mine = pl.ds(pl.multiple_of(p * R, 16), R)
+            core_out[sl] = dot(u[theirs, place], right).astype(bf16)
+
+            @pl.when(k == 0)
+            def _():
+                pl.semaphore_wait(ready.at[0], 1)
+
+            core_copy(k).start()
+            keep[lax.rem(k, keeps)] = dot(u[mine, place], right)
+
+        @pl.when(k < first_kind)
+        def _():
+            products(place_d, flat(buf_a, column(k + (wide - own) * (1 - odd), C)))
+
+        @pl.when(k >= first_kind)
+        def _():
+            products(place_x, flat(buf_b, column(k - first_kind, C)))
+
+    def fetch(k):
+        c = k - count
+
+        @pl.when(c < cross)
+        def _():
             cross_copy(c).wait_recv()
             keep[lax.rem(k, keeps)] = ut[cross_place(c)].astype(f32)
-            w[slot(k)] = jnp.zeros((R, C), bf16)
-
-        c_cross = k - 1
-
-        @pl.when((c_cross >= 0) & (c_cross < pre))
-        def _():
-            core_copy(c_cross).wait_recv()
-            both = keep[lax.rem(c_cross, keeps)] + w[slot(c_cross)].astype(f32)
-            cross_out[c_cross] = both.astype(bf16)
-            cross_copy(c_cross).start()
+
+        @pl.when(c == cross)
+        def _():
+            spare_copy().wait_recv()
+            keep[lax.rem(k, keeps)] = u[spare].astype(f32)
+
+        w[slot(k)] = jnp.zeros((R, C), bf16)
+
+    def ship(c):
+        core_copy(c).wait_recv()
+        both = keep[lax.rem(c, keeps)] + w[slot(c)].astype(f32)
+        cross_out[c] = both.astype(bf16)
+
+        @pl.when(c < cross)
+        def _():
+            cross_copy(c).start()
+
+        @pl.when(c == cross)
+        def _():
+            spare_copy().start()
+
+    def step(own_pass, lo, hi, k, carry):
+        if own_pass:
+            @pl.when(k < count)
+            def _():
+                make(k)
+
+            @pl.when((k >= 1) & (k - 1 < pre))
+            def _():
+                ship(k - 1)
+        else:
+            @pl.when(k < count + came)
+            def _():
+                fetch(k)
 
         n_near = k - 1 - pre - near
 
-        @pl.when((n_near >= lo) & (n_near < hi) & (n_near + pre < count))
-        def _():
-            core_copy(n_near + pre).wait_recv()
+        if own_pass:
+            @pl.when((n_near >= lo) & (n_near < hi))
+            def _():
+                core_copy(n_near + pre).wait_recv()
 
         n_up = k - 1 - pre - z
 
@@ -425,9 +463,9 @@
         return carry
 
     own_lines = count - pre
-    lax.fori_loop(0, count + 1 + far, functools.partial(step, 0, own_lines), 0)
+    lax.fori_loop(0, count + 1 + far, functools.partial(step, True, 0, own_lines), 0)
     later = jnp.where(s == 2, count + came + 1 + far, count)
-    lax.fori_loop(count, later, functools.partial(step, count, count + came), 0)
+    lax.fori_loop(count, later, functools.partial(step, False, count, count + came), 0)
 
     for back in (2, 1):
         core_copy(count - back).wait_send()
@@ -447,6 +485,8 @@
     def _():
         for c in range(cross):
             cross_copy(c).wait_send()
+        spare_copy().wait_send()
+        away_arrival(cross).wait_recv()
 
     @pl.when(odd == 0)
     def _():
@@ -480,7 +520,7 @@
     bias_ref,
     gain_ref,
     shift_ref,
-    draws_ref,
+    draws_hbm,
     out_hbm,
     grad_hbm,
     g_hbm,
@@ -489,7 +529,7 @@
     M, L, LP, D, FF, HD, FE, NS, ND, fscale, in_kernel, C = cfg
     small_outs = refs[:3] if in_kernel else ()
     small_ref = refs[3] if in_kernel else refs[0]
-    fmap_ref = refs[4] if in_kernel else refs[1]
+    fmap_ref, draws_ref = refs[4:6] if in_kernel else refs[1:3]
     (
         w,
         u,
@@ -518,7 +558,7 @@
         stage_sem,
         g_sem,
         *reduce_refs,
-    ) = refs[5:] if in_kernel else refs[2:]
+    ) = refs[6:] if in_kernel else refs[3:]
     HALF = FF // 2
     GH = 256 // HD
     G = D // 256
@@ -537,9 +577,8 @@
     last = s == NS - 1
     sib = d + 1 - 2 * lax.rem(d, 2)
     mate = d + 2 - 4 * lax.rem(d // 2, 2)
-    quarter = D // 4
     pieces = 4
-    piece = quarter // pieces
+    piece = D // 12
 
     barrier = pltpu.get_barrier_semaphore()
 
@@ -571,6 +610,12 @@
         slab_hbm.at[0, :, pl.ds(FF, HALF)], u.at[:, pl.ds(HALF, HALF)], load_sem.at[1]
     )
     w_copy.start()
+    draws_copy = pltpu.make_async_copy(draws_hbm, draws_ref, load_sem.at[2])
+
+    @pl.when(is_attn)
+    def _():
+        draws_copy.start()
+
 
     def land_copy(ref, m):
         sl = lax.rem(m, 2)
@@ -603,35 +648,62 @@
     def _():
         pl.semaphore_wait(barrier, partners + 2 + extra)
 
-    q0 = lax.rem(d, 4)
-    q1 = q0 + 2 - 4 * (q0 // 2)
     left = pl.ds(0, HALF)
-
-    def u_rows(q, i):
-        return pl.ds(pl.multiple_of(q * quarter + i * piece, piece), piece)
+    core = lax.rem(d, 2)
+    side = lax.rem(d // 2, 2)
+
+    def u_rows(i, side=side):
+        n = jnp.where(i < 2, 8 * side, 0) + 2 * i + core
+        return pl.ds(pl.multiple_of(n * piece, piece), piece)
 
     def u_from_section(i):
         return pltpu.make_async_remote_copy(
-            slab_hbm.at[0, u_rows(q0, i), pl.ds(FF, HALF)],
-            u.at[u_rows(q0, i), left],
+            slab_hbm.at[0, u_rows(i), pl.ds(FF, HALF)],
+            u.at[u_rows(i), left],
             u_send.at[0, i],
             u_recv.at[0, i],
             device_id=(s + 1, d),
             device_id_type=MESH,
         )
 
-    def u_copy_to(q, i, k, to):
+    def u_copy_to(rows, i, k, to):
         return pltpu.make_async_remote_copy(
-            u.at[u_rows(q, i), left],
-            u.at[u_rows(q, i), left],
+            u.at[rows, left],
+            u.at[rows, left],
             u_send.at[k, i],
             u_recv.at[k, i],
             device_id=(s, to),
             device_id_type=MESH,
         )
 
-    @pl.when(is_attn & (s < NS - 1))
-    def _():
+    detour = (2, 3) if NS == 4 else ()
+
+    def u_aside(i, to, k):
+        src = slab_hbm.at[0, u_rows(i), pl.ds(FF, HALF)] if k == 0 else u.at[u_rows(i), left]
+        return pltpu.make_async_remote_copy(
+            src,
+            u.at[u_rows(i), left],
+            u_send.at[k, i],
+            u_recv.at[0, i],
+            device_id=(to, d),
+            device_id_type=MESH,
+        )
+
+    @pl.when(first)
+    def _():
+        for i in range(pieces):
+            if i in detour:
+                u_aside(i, 2, 0).start()
+            else:
+                u_from_section(i).start()
+
+    @pl.when(is_attn & (s > 0) & (s < NS - 1))
+    def _():
+        for i in detour:
+            u_aside(i, 1, 1).wait_recv()
+            u_aside(i, 1, 1).start()
+        for i in detour:
+            u_aside(i, 1, 1).wait_send()
         for i in range(pieces):
             u_from_section(i).start()
 
@@ -645,6 +717,7 @@
     @pl.when(is_attn)
     def _():
         turn(w, wt, 3 * D // 256, D // 256)
+        draws_copy.wait()
         f_row = lax.broadcasted_iota(jnp.int32, (FE, GF), 0)
         f_col = lax.broadcasted_iota(jnp.int32, (FE, GF), 1)
         for n in range(G * GH):
@@ -663,16 +736,16 @@
         turn(u, ut, HALF // 256, HALF // 256)
         for i in range(pieces):
             u_from_section(i).wait_recv()
-            u_copy_to(q0, i, 1, mate).start()
-            u_copy_to(q0, i, 2, sib).start()
-            if i > 0:
-                u_copy_to(q0, i - 1, 1, mate).wait_recv()
-                u_copy_to(q1, i - 1, 3, sib).start()
-        u_copy_to(q0, pieces - 1, 1, mate).wait_recv()
-        u_copy_to(q1, pieces - 1, 3, sib).start()
+            if i < 2:
+                u_copy_to(u_rows(i), i, 1, mate).start()
+            u_copy_to(u_rows(i), i, 2, sib).start()
+            if i >= 2:
+                u_copy_to(u_rows(i - 2, 1 - side), i - 2, 1, mate).wait_recv()
+                u_copy_to(u_rows(i - 2, 1 - side), i - 2, 3, sib).start()
         for i in range(pieces):
-            u_copy_to(q0, i, 2, sib).wait_recv()
-            u_copy_to(q1, i, 3, sib).wait_recv()
+            u_copy_to(u_rows(i), i, 2, sib).wait_recv()
+        for i in range(2):
+            u_copy_to(u_rows(i, 1 - side), i, 3, sib).wait_recv()
         turn(u, ut, 0, HALF // 256)
 
     g_row = gain_ref[...]
@@ -948,7 +1021,7 @@
 
         if mode > 0:
             write_out(out_copy, out, out_stage, m)
-        if mode == 1:
+        if mode > 0:
             @pl.when(first & (m == M - 1))
             def _():
                 turn(w, wt, 0, 3 * D // 256)
@@ -1004,7 +1077,7 @@
             def _():
                 act(m, 2)
 
-            for h in range(2):
+            for h in range(2 if SPLIT else 0):
                 @pl.when(here & apart & (lax.rem(i, 2) == h))
                 def _():
                     act(m, h)
@@ -1038,9 +1111,10 @@
     @pl.when(is_ff)
     def _():
         for i in range(pieces):
-            u_copy_to(q0, i, 1, mate).wait_send()
-            u_copy_to(q0, i, 2, sib).wait_send()
-            u_copy_to(q1, i, 3, sib).wait_send()
+            u_copy_to(u_rows(i), i, 2, sib).wait_send()
+        for i in range(2):
+            u_copy_to(u_rows(i), i, 1, mate).wait_send()
+            u_copy_to(u_rows(i, 1 - side), i, 3, sib).wait_send()
 
     if in_kernel:
         reduce_gradients(
@@ -1105,6 +1179,7 @@
     scratch = [pltpu.VMEM((1, small_size), f32)] if in_kernel else []
     scratch += [
         pltpu.VMEM((G, GH * HD, GF), bf16),
+        pltpu.VMEM((H, HD, FE), jnp.int32),
         pltpu.VMEM((D, FF), bf16),
         pltpu.VMEM((D, FF), bf16),
         pltpu.VMEM((FF, D), bf16),
@@ -1121,7 +1196,7 @@
         pltpu.VMEM((2, L, D), bf16),
         pltpu.VMEM((L, D), bf16),
         pltpu.VMEM((L, D), bf16),
-        dma((2,)),
+        dma((3,)),
         dma((2,)),
         dma((4, 4)),
         dma((4, 4)),
@@ -1140,7 +1215,7 @@
             pltpu.SemaphoreType.REGULAR((3,)),
             pltpu.VMEM((Z + 1, Z * B, C), f32),
             pltpu.VMEM((2, Z * B, C), bf16),
-            pltpu.VMEM((cross, Z * B, C), bf16),
+            pltpu.VMEM((cross + 1, Z * B, C), bf16),
             pltpu.VMEM((2, Z, B, C), bf16),
             pltpu.VMEM((2, B, C), f32),
             pltpu.VMEM((ND, 1, small_size), f32),
@@ -1150,10 +1225,10 @@
             dma((lines, Z)),
             dma((lines, Z)),
             dma((2,)),
-            dma((cross,)),
-            dma((cross,)),
-            dma((cross,)),
-            dma((cross,)),
+            dma((cross + 1,)),
+            dma((cross + 1,)),
+            dma((cross + 1,)),
+            dma((cross + 1,)),
             dma((ND,)),
             dma((ND,)),
         ]
@@ -1169,7 +1244,7 @@
             jax.ShapeDtypeStruct(g_shape, f32),
         ]
         + [jax.ShapeDtypeStruct((1, n), f32) for n in smalls],
-        in_specs=[smem, hbm, hbm, vmem, hbm, vmem, vmem, vmem, vmem],
+        in_specs=[smem, hbm, hbm, vmem, hbm, vmem, vmem, vmem, hbm],
         out_specs=[hbm, hbm, hbm] + [vmem] * len(smalls),
         scratch_shapes=scratch,
         compiler_params=pltpu.CompilerParams(

time: 200 us -> 196 us (0.980)
  Pallas kernels: 189 us -> 185 us
    pallas_call x1, Pallas kernels: 189 us -> 185 us  [shards(): pl.pallas_call(functools.partial(pipeline_kernel, cfg), out_shape=[jax.Sh...]
where the time goes in v1:
time: 196 us; the launch traced here: 195 us
  Pallas kernels  185 us (94%)
  local copies, waits for them, and re-layouts  9.87 us (5%)
    pallas_call x1, Pallas kernels, shards(): pl.pallas_call(functools.partial(pipeline_kernel, cfg), out_shape=[jax.Sh...  185 us
    unnamed x17, local copies, waits for them, and re-layouts  9.87 us

profile of v1, /device:TPU:2, one launch (start us, length us, event | category | flops | bytes accessed | tf_op | source)
XLA Modules:
  0.0 195.4 jit_solution(11902195268054590177)
XLA Ops:
  0.6 1.8 copy.15.draws_hbm
  2.5 184.9 %pipeline.1 = (bf16[6,202,768]{2,1,0:T(8,128)(2,1)}, bf16[6,202,768]{2,1,0:T(8,128)(2,1)}, f32[96,4608]{1,0:T(8,128)}, f32[1,384]{1,0:T(1,128)}, f32[1,96]{1,0:T(1,128)}, /*index=5*/f32[1,96]{1,0:T(1,128)}) custom-call(s32[6]{0:T(128)} %len_ref.1, bf16[6,202,768]{2,1,0:T(8,128)(2,1)} %x_hbm.1, bf16[6,202,768]{2,1,0:T(8,128)(2,1)} %cot_hbm.1, ...), custom_call_target="tpu_custom_call" | custom-call | tf_op jit(solution)/shard_map/pipeline/pallas_call | solution.py:1239
  187.4 0.0 copy-start
  187.4 3.0 %copy.22 = bf16[1,6,202,768]{3,2,1,0:T(8,128)(2,1)} copy(bf16[1,6,202,768]{3,2,1,0:T(8,128)(2,1)} %bitcast.4) | data formatting | bytes 3723264
  190.4 0.0 copy-done
  190.4 0.0 copy-start.1
  190.4 1.3 copy.23
  191.7 0.9 copy-done.1
  192.6 0.0 copy-start.2
  192.6 0.0 copy-start.4
  192.6 0.0 copy-start.3
  192.6 1.2 copy.24
  193.8 0.0 copy-done.2
  193.8 0.6 copy.25
  194.4 0.0 copy-done.4
  194.4 0.5 copy.26
  194.9 0.0 copy-done.3
  194.9 0.5 copy.27
Async XLA Ops:
  187.4 3.1 %copy-start = (bf16[6,202,768]{2,1,0:T(8,128)(2,1)S(1)}, bf16[6,202,768]{2,1,0:T(8,128)(2,1)}, u32[]{:S(2)}) copy-start(bf16[6,202,768]{2,1,0:T(8,128)(2,1)} %get-tuple-element.13) | copy-start | bytes 5584900
  190.4 2.2 %copy-start.1 = (f32[96,4608]{1,0:T(8,128)S(1)}, f32[96,4608]{1,0:T(8,128)}, u32[]{:S(2)}) copy-start(f32[96,4608]{1,0:T(8,128)} %get-tuple-element.14) | copy-start | bytes 5308420
  192.6 1.2 copy-start.2
  192.6 1.8 copy-start.4
  192.6 2.3 %copy-start.3 = (f32[1,96]{1,0:T(1,128)S(1)}, f32[1,96]{1,0:T(1,128)}, u32[]{:S(2)}) copy-start(f32[1,96]{1,0:T(1,128)} %get-tuple-element.29) | copy-start | bytes 1156

commit v2 on v1

--- a/solution.py
+++ b/solution.py
@@ -722,7 +722,7 @@
         f_col = lax.broadcasted_iota(jnp.int32, (FE, GF), 1)
         for n in range(G * GH):
             shift = jnp.where(f_col == f_row + n % GH * FE, 1.0, 0.0).astype(bf16)
-            spread = dot(draws_ref[n].astype(f32).astype(bf16), shift)
+            spread = dot_rows(draws_ref[n].astype(f32).astype(bf16), shift)
             fmap_ref[n // GH, pl.ds(n % GH * HD, HD), :] = spread.astype(bf16)
 
     @pl.when(s == 2)
@@ -1152,6 +1152,28 @@
     grad_copy(M - 1).wait()
 
 
+def place_results(*refs):
+    count = (len(refs) - 1) // 3
+    sems = refs[-1]
+    inward, outward = [], []
+    for src, dst, mid in zip(refs[:count], refs[count : 2 * count], refs[2 * count : 3 * count]):
+        parts = [(slice(None),)]
+        if src.shape[0] > 1:
+            step = src.shape[0] // 6
+            parts = [(pl.ds(i * step, step),) for i in range(6)]
+        for part in parts:
+            n = len(inward)
+            inward.append(pltpu.make_async_copy(src.at[part], mid.at[part], sems.at[0, n]))
+            outward.append(pltpu.make_async_copy(mid.at[part], dst.at[part], sems.at[1, n]))
+    for copy in inward:
+        copy.start()
+    for first, second in zip(inward, outward):
+        first.wait()
+        second.start()
+    for copy in outward:
+        copy.wait()
+
+
 def shards(
     block_input, cotangent, lengths, predicted, slab, in_bias, norm_gain, norm_bias, feature_draws
 ):
@@ -1179,7 +1201,7 @@
     scratch = [pltpu.VMEM((1, small_size), f32)] if in_kernel else []
     scratch += [
         pltpu.VMEM((G, GH * HD, GF), bf16),
-        pltpu.VMEM((H, HD, FE), jnp.int32),
+        pltpu.VMEM((H, FE, HD), jnp.int32),
         pltpu.VMEM((D, FF), bf16),
         pltpu.VMEM((D, FF), bf16),
         pltpu.VMEM((FF, D), bf16),
@@ -1260,11 +1282,19 @@
         in_bias,
         norm_gain,
         norm_bias,
-        feature_draws,
+        jnp.swapaxes(feature_draws, 1, 2),
     )
     if in_kernel:
-        own = grads
-        parts = small
+        results = (section_out, section_grad, grads, *small)
+        section_out, section_grad, own, *parts = pl.pallas_call(
+            place_results,
+            out_shape=[jax.ShapeDtypeStruct(r.shape, r.dtype) for r in results],
+            in_specs=[hbm] * len(results),
+            out_specs=[hbm] * len(results),
+            scratch_shapes=[pltpu.VMEM(r.shape, r.dtype) for r in results] + [dma((2, 6 * len(results)))],
+            compiler_params=pltpu.CompilerParams(vmem_limit_bytes=62 * 2**20),
+            name="place_results",
+        )(*results)
     else:
         def scatter(value):
             return lax.psum_scatter(value, "dp", scatter_dimension=0, tiled=True)

time: 196 us -> 191 us (0.974)
  local copies, waits for them, and re-layouts: 9.87 us -> 0 us
  Pallas kernels: 185 us -> 190 us
    unnamed x17 -> x0, local copies, waits for them, and re-layouts: 9.87 us -> none
    pallas_call x0 -> x1, Pallas kernels: none -> 5.51 us  [shards(): pl.pallas_call(place_results, out_shape=[jax.ShapeDtypeStruct(r.shape, r....]
where the time goes in v2:
time: 191 us
  Pallas kernels  190 us (99%)
    pallas_call x1, Pallas kernels, shards(): pl.pallas_call(functools.partial(pipeline_kernel, cfg), out_shape=[jax.Sh...  185 us
    pallas_call x1, Pallas kernels, shards(): pl.pallas_call(place_results, out_shape=[jax.ShapeDtypeStruct(r.shape, r....  5.51 us

profile of v2, /device:TPU:2, one launch (start us, length us, event | category | flops | bytes accessed | tf_op | source)
XLA Modules:
  0.0 191.2 jit_solution(17611548495058252456)
XLA Ops:
  0.6 184.9 %pipeline.1 = (bf16[6,202,768]{2,1,0:T(8,128)(2,1)}, bf16[6,202,768]{2,1,0:T(8,128)(2,1)}, f32[96,4608]{1,0:T(8,128)}, f32[1,384]{1,0:T(1,128)}, f32[1,96]{1,0:T(1,128)}, /*index=5*/f32[1,96]{1,0:T(1,128)}) custom-call(s32[6]{0:T(128)} %len_ref.1, bf16[6,202,768]{2,1,0:T(8,128)(2,1)} %x_hbm.1, bf16[6,202,768]{2,1,0:T(8,128)(2,1)} %cot_hbm.1, ...), custom_call_target="tpu_custom_call" | custom-call | tf_op jit(solution)/shard_map/pipeline/pallas_call | solution.py:1261
  185.5 5.5 %place_results.1 = (bf16[6,202,768]{2,1,0:T(8,128)(2,1)}, bf16[6,202,768]{2,1,0:T(8,128)(2,1)}, f32[96,4608]{1,0:T(8,128)}, f32[1,384]{1,0:T(1,128)}, f32[1,96]{1,0:T(1,128)}, /*index=5*/f32[1,96]{1,0:T(1,128)}) custom-call(bf16[6,202,768]{2,1,0:T(8,128)(2,1)} %get-tuple-element.18.refs_0_, bf16[6,202,768]{2,1,0:T(8,128)(2,1)} %get-tuple-element.19.refs_1_, ...), custom_call_target="tpu_custom_call" | custom-call | tf_op jit(solution)/shard_map/place_results/pallas_call | solution.py:1289

commit v3 on v2

--- a/solution.py
+++ b/solution.py
@@ -235,18 +235,18 @@
 
     def up_copy(n, zt):
         return dma_to(
-            line_out.at[lax.rem(n, 2), zt],
+            line_out.at[lax.rem(n, 3), zt],
             ut.at[line_place(n, zt)],
-            line_send.at[lax.rem(n, 2), zt],
+            line_send.at[lax.rem(n, 3), zt],
             up_recv.at[n, zt],
             device_id=(s, d + 2),
         )
 
     def down_copy(n, zt):
         return dma_to(
-            line_out.at[lax.rem(n, 2), zt],
+            line_out.at[lax.rem(n, 3), zt],
             wt.at[line_place(n, zt)],
-            line_send.at[lax.rem(n, 2), zt],
+            line_send.at[lax.rem(n, 3), zt],
             down_recv.at[n, zt],
             device_id=(s, d - 2),
         )
@@ -385,20 +385,20 @@
             for zt in range(Z - 1, 0, -1):
                 @pl.when(zt > z)
                 def _():
-                    @pl.when(n_up >= 2)
+                    @pl.when(n_up >= 3)
                     def _():
-                        up_copy(n_up - 2, zt).wait_send()
+                        up_copy(n_up - 3, zt).wait_send()
 
                     @pl.when(z > 0)
                     def _():
                         up_copy(n_up, zt).wait_recv()
-                        line_out[lax.rem(n_up, 2), zt] = (
+                        line_out[lax.rem(n_up, 3), zt] = (
                             total(n_up, zt) + ut[line_place(n_up, zt)].astype(f32)
                         ).astype(bf16)
 
                     @pl.when(z == 0)
                     def _():
-                        line_out[lax.rem(n_up, 2), zt] = total(n_up, zt).astype(bf16)
+                        line_out[lax.rem(n_up, 3), zt] = total(n_up, zt).astype(bf16)
 
                     up_copy(n_up, zt).start()
 
@@ -413,20 +413,20 @@
             for zt in range(Z - 1):
                 @pl.when(zt < z)
                 def _():
-                    @pl.when(n_down >= 2)
+                    @pl.when(n_down >= 3)
                     def _():
-                        down_copy(n_down - 2, zt).wait_send()
+                        down_copy(n_down - 3, zt).wait_send()
 
                     @pl.when(z < Z - 1)
                     def _():
                         down_copy(n_down, zt).wait_recv()
-                        line_out[lax.rem(n_down, 2), zt] = (
+                        line_out[lax.rem(n_down, 3), zt] = (
                             total(n_down, zt) + wt[line_place(n_down, zt)].astype(f32)
                         ).astype(bf16)
 
                     @pl.when(z == Z - 1)
                     def _():
-                        line_out[lax.rem(n_down, 2), zt] = total(n_down, zt).astype(bf16)
+                        line_out[lax.rem(n_down, 3), zt] = total(n_down, zt).astype(bf16)
 
                     down_copy(n_down, zt).start()
 
@@ -467,8 +467,7 @@
     later = jnp.where(s == 2, count + came + 1 + far, count)
     lax.fori_loop(count, later, functools.partial(step, False, count, count + came), 0)
 
-    for back in (2, 1):
-        core_copy(count - back).wait_send()
+    for back in (3, 2, 1):
         n = lines - back
         for zt in range(Z):
             @pl.when(zt > z)
@@ -479,7 +478,9 @@
             def _():
                 down_copy(n, zt).wait_send()
 
-        final_wait(n)
+    for back in (2, 1):
+        core_copy(count - back).wait_send()
+        final_wait(lines - back)
 
     @pl.when(s == 1)
     def _():
@@ -1238,12 +1239,12 @@
             pltpu.VMEM((Z + 1, Z * B, C), f32),
             pltpu.VMEM((2, Z * B, C), bf16),
             pltpu.VMEM((cross + 1, Z * B, C), bf16),
-            pltpu.VMEM((2, Z, B, C), bf16),
+            pltpu.VMEM((3, Z, B, C), bf16),
             pltpu.VMEM((2, B, C), f32),
             pltpu.VMEM((ND, 1, small_size), f32),
             dma((2,)),
             dma((chunks,)),
-            dma((2, Z)),
+            dma((3, Z)),
             dma((lines, Z)),
             dma((lines, Z)),
             dma((2,)),

time: 191 us -> 191 us (level)
  no operation moved by 1% of the time
where the time goes in v3:
time: 191 us
  Pallas kernels  190 us (99%)
    pallas_call x1, Pallas kernels, shards(): pl.pallas_call(functools.partial(pipeline_kernel, cfg), out_shape=[jax.Sh...  185 us
    pallas_call x1, Pallas kernels, shards(): pl.pallas_call(place_results, out_shape=[jax.ShapeDtypeStruct(r.shape, r....  5.51 us

profile of v3, /device:TPU:2, one launch (start us, length us, event | category | flops | bytes accessed | tf_op | source)
XLA Modules:
  0.0 191.3 jit_solution(8114699808177657495)
XLA Ops:
  0.6 185.0 %pipeline.1 = (bf16[6,202,768]{2,1,0:T(8,128)(2,1)}, bf16[6,202,768]{2,1,0:T(8,128)(2,1)}, f32[96,4608]{1,0:T(8,128)}, f32[1,384]{1,0:T(1,128)}, f32[1,96]{1,0:T(1,128)}, /*index=5*/f32[1,96]{1,0:T(1,128)}) custom-call(s32[6]{0:T(128)} %len_ref.1, bf16[6,202,768]{2,1,0:T(8,128)(2,1)} %x_hbm.1, bf16[6,202,768]{2,1,0:T(8,128)(2,1)} %cot_hbm.1, ...), custom_call_target="tpu_custom_call" | custom-call | tf_op jit(solution)/shard_map/pipeline/pallas_call | solution.py:1262
  185.6 5.5 %place_results.1 = (bf16[6,202,768]{2,1,0:T(8,128)(2,1)}, bf16[6,202,768]{2,1,0:T(8,128)(2,1)}, f32[96,4608]{1,0:T(8,128)}, f32[1,384]{1,0:T(1,128)}, f32[1,96]{1,0:T(1,128)}, /*index=5*/f32[1,96]{1,0:T(1,128)}) custom-call(bf16[6,202,768]{2,1,0:T(8,128)(2,1)} %get-tuple-element.18.refs_0_, bf16[6,202,768]{2,1,0:T(8,128)(2,1)} %get-tuple-element.19.refs_1_, ...), custom_call_target="tpu_custom_call" | custom-call | tf_op jit(solution)/shard_map/place_results/pallas_call | solution.py:1290
